TPU v7x, 512 devices: a whole 4x8x8 slice. The times are simulated.
512 devices in a mesh: sims: 32 (over z_lo, y, core), sites: 16 (over x, z_hi).
Axes of the slice: x: 4, y: 8, z: 8 (z_hi: 4, z_lo: 2; z = z_hi * 2 + z_lo), core: 2. Of those that a mesh axis runs over, the one named last changes fastest.
Arguments:
- genotypes: int32 [32, 64, 8192], P('sims', None, 'sites'), may hold values from 0 to 1
- key_prior: bfloat16 [32, 2048], P('sims', 'sites'), may hold values from -300 to 300
- band_reach: int32 [32], P('sims'), may hold values from 128 to 512, as said below
- cotangent: bfloat16 [32, 2048, 512], P('sims', 'sites'), may hold values from -0.09375 to 0.09375
- conv_weight: float32 [4, 64], replicated, may hold values from -3 to 3
- conv_bias: float32 [64], replicated, may hold values from -3 to 3
- mix_weight: float32 [3, 64, 64], replicated, may hold values from -0.4375 to 0.4375
- embed_weight: float32 [64, 512], replicated, may hold values from -0.75 to 0.75
- norm_gain: float32 [512], replicated, may hold values from 0.5 to 1.5
- attn_weight: bfloat16 [4, 512, 512], replicated, may hold values from -0.25 to 0.25
Outputs:
- grad_attention: float32 [1048576], P(('sims', 'sites'))
- grad_conv: float32 [4, 64], replicated
- grad_bias: float32 [64], replicated
- grad_mix: float32 [3, 64, 64], replicated
- grad_embed: float32 [64, 512], replicated
- grad_gain: float32 [512], replicated
Inputs may be any that keep to these rules, and one draw needn't show every extreme that they name: `band_reach`: some evolution has reach exactly 512 in every draw.
All inputs are finite; a program needn't handle non-finite values.
Results may differ from a plain program's by a relative error of at most 0.017.
Values may be sent and summed in bfloat16 or wider, within the bound.
A program may use at most 64 MiB of HBM per device.

v0:
```python
import jax
import jax.numpy as jnp
from jax import lax
from jax.sharding import PartitionSpec as P

HEADS = 8
HEAD_DIM = 64
BAND = 512
HIGH = lax.Precision.HIGHEST
EPS = 1e-06


def extended(cells, sides, width):
    for axis, dim in sides:
        count = lax.axis_size(axis)
        head = lax.slice_in_dim(cells, 0, width, axis=dim)
        tail = lax.slice_in_dim(cells, cells.shape[dim] - width, cells.shape[dim], axis=dim)
        cells = jnp.concatenate(
            [
                lax.ppermute(tail, axis, [(i, (i + 1) % count) for i in range(count)]),
                cells,
                lax.ppermute(head, axis, [((i + 1) % count, i) for i in range(count)]),
            ],
            axis=dim,
        )
    return cells


def from_behind(value, axis, steps):
    count = lax.axis_size(axis)
    pairs = [(source, (source + steps) % count) for source in range(count)]
    return lax.ppermute(value, axis, pairs)


def silu_slope(value):
    sigma = jax.nn.sigmoid(value)
    return sigma * (1.0 + value * (1.0 - sigma))


def block_offsets(count, reach_blocks):
    chosen = []
    taken = []
    for distance in range(reach_blocks + 1):
        for offset in (distance, -distance):
            if offset % count not in taken:
                taken.append(offset % count)
                chosen.append(offset)
    return chosen


def split_heads(array, heads):
    return array.reshape(array.shape[0], array.shape[1], heads, array.shape[2] // heads)


def band_scores(query, keys, prior, query_places, key_places, limit, cycle_tokens, factor):
    scores = jnp.einsum("sqhe,skhe->shqk", query, keys, preferred_element_type=jnp.float32) * factor
    scores = scores + prior.astype(jnp.float32)[:, None, None, :]
    apart = (key_places[None, :] - query_places[:, None]) % cycle_tokens
    apart = jnp.minimum(apart, cycle_tokens - apart)
    inside = apart[None, None] <= limit[:, None, None, None]
    return (scores, inside)


def per_device(
    genotypes,
    key_prior,
    band_reach,
    cotangent,
    conv_weight,
    conv_bias,
    mix_weight,
    embed_weight,
    norm_gain,
    attn_weight,
):
    sims, haps, sites = genotypes.shape
    patch = conv_weight.shape[0]
    local = sites // patch
    width = attn_weight.shape[1]
    heads = HEADS
    factor = HEAD_DIM ** (-0.5)
    count = lax.axis_size("sites")
    cycle_tokens = local * count
    place = lax.axis_index("sites")
    ordinal = jnp.arange(local, dtype=jnp.int32)
    patches = genotypes.astype(jnp.float32).reshape(sims, haps, local, patch)
    pre = (
        jnp.einsum("shtk,kc->shct", patches, conv_weight, precision=HIGH)
        + conv_bias[None, None, :, None]
    )
    pooled = jnp.mean(jax.nn.silu(pre), axis=1)
    pooled_wide = extended(pooled, (("sites", 2),), 1)
    mixed = jnp.zeros((sims, mix_weight.shape[2], local), jnp.float32)
    for shift_by in (-1, 0, 1):
        mixed = mixed + jnp.einsum(
            "co,sct->sot",
            mix_weight[shift_by + 1],
            pooled_wide[:, :, 1 + shift_by : 1 + shift_by + local],
            precision=HIGH,
        )
    activated = jax.nn.silu(mixed)
    embedded = jnp.einsum("sct,cd->std", activated, embed_weight, precision=HIGH).astype(
        jnp.bfloat16
    )
    wide = embedded.astype(jnp.float32)
    inverse = lax.rsqrt(jnp.mean(wide * wide, axis=2, keepdims=True) + EPS)
    normed = (wide * inverse * norm_gain).astype(jnp.bfloat16)
    query = jnp.einsum(
        "std,de->ste", normed, attn_weight[0], preferred_element_type=jnp.float32
    ).astype(jnp.bfloat16)
    keys = jnp.einsum(
        "std,de->ste", normed, attn_weight[1], preferred_element_type=jnp.float32
    ).astype(jnp.bfloat16)
    values = jnp.einsum(
        "std,de->ste", normed, attn_weight[2], preferred_element_type=jnp.float32
    ).astype(jnp.bfloat16)
    query_heads = split_heads(query, heads)
    key_heads = split_heads(keys, heads)
    value_heads = split_heads(values, heads)
    reach_blocks = -(-BAND // local)
    offsets = block_offsets(count, reach_blocks)
    packed = jnp.concatenate([keys, values, key_prior[:, :, None]], axis=2)
    gathered = {0: packed}
    for offset in offsets[1:]:
        gathered[offset] = from_behind(packed, "sites", -offset)
    packed_cat = jnp.concatenate([gathered[offset] for offset in offsets], axis=1)
    key_cat = split_heads(packed_cat[:, :, :width], heads)
    value_cat = split_heads(packed_cat[:, :, width : 2 * width], heads)
    prior_cat = packed_cat[:, :, 2 * width]
    key_places = jnp.concatenate([(place + offset) % count * local + ordinal for offset in offsets])
    query_places = place * local + ordinal
    scores, inside = band_scores(
        query_heads, key_cat, prior_cat, query_places, key_places, band_reach, cycle_tokens, factor
    )
    row_top = jnp.max(jnp.where(inside, scores, -jnp.inf), axis=-1, keepdims=True)
    lifted = jnp.where(inside, jnp.exp(scores - row_top), 0.0)
    row_total = jnp.sum(lifted, axis=-1, keepdims=True)
    prob = lifted / row_total
    prob_half = prob.astype(jnp.bfloat16)
    attended_full = jnp.einsum(
        "shqk,skhe->sqhe", prob_half, value_cat, preferred_element_type=jnp.float32
    )
    attended = attended_full.astype(jnp.bfloat16).reshape(sims, local, width)
    grad_attended = jnp.einsum(
        "std,ed->ste", cotangent, attn_weight[3], preferred_element_type=jnp.float32
    ).astype(jnp.bfloat16)
    grad_heads = split_heads(grad_attended, heads)
    delta = jnp.einsum("sqhe,sqhe->shq", grad_heads.astype(jnp.float32), attended_full)
    grad_prob = jnp.einsum(
        "sqhe,skhe->shqk", grad_heads, value_cat, preferred_element_type=jnp.float32
    )
    grad_scores = (prob * (grad_prob - delta[..., None]) * factor).astype(jnp.bfloat16)
    grad_query = jnp.einsum(
        "shqk,skhe->sqhe", grad_scores, key_cat, preferred_element_type=jnp.float32
    ).astype(jnp.bfloat16)
    grad_query = grad_query.reshape(sims, local, width)
    key_part = jnp.einsum(
        "shqk,sqhe->skhe", grad_scores, query_heads, preferred_element_type=jnp.float32
    )
    value_part = jnp.einsum(
        "shqk,sqhe->skhe", prob_half, grad_heads, preferred_element_type=jnp.float32
    )
    key_sum = key_part[:, 0:local]
    value_sum = value_part[:, 0:local]
    for position, offset in enumerate(offsets[1:], start=1):
        lower = position * local
        both = jnp.concatenate(
            [key_part[:, lower : lower + local], value_part[:, lower : lower + local]], axis=2
        ).astype(jnp.bfloat16)
        back = from_behind(both, "sites", offset).astype(jnp.float32)
        key_sum = key_sum + back[:, :, :heads]
        value_sum = value_sum + back[:, :, heads:]
    grad_keys = key_sum.astype(jnp.bfloat16).reshape(sims, local, width)
    grad_values = value_sum.astype(jnp.bfloat16).reshape(sims, local, width)
    term_query = jnp.einsum("std,ste->de", normed, grad_query, preferred_element_type=jnp.float32)
    term_keys = jnp.einsum("std,ste->de", normed, grad_keys, preferred_element_type=jnp.float32)
    term_values = jnp.einsum("std,ste->de", normed, grad_values, preferred_element_type=jnp.float32)
    term_output = jnp.einsum("std,ste->de", attended, cotangent, preferred_element_type=jnp.float32)
    flat_terms = jnp.stack([term_query, term_keys, term_values, term_output]).reshape(-1)
    grad_attention = lax.psum_scatter(
        lax.psum_scatter(flat_terms, "sims", scatter_dimension=0, tiled=True),
        "sites",
        scatter_dimension=0,
        tiled=True,
    )
    grad_normed = jnp.einsum(
        "ste,de->std", grad_query, attn_weight[0], preferred_element_type=jnp.float32
    )
    grad_normed = grad_normed + jnp.einsum(
        "ste,de->std", grad_keys, attn_weight[1], preferred_element_type=jnp.float32
    )
    grad_normed = grad_normed + jnp.einsum(
        "ste,de->std", grad_values, attn_weight[2], preferred_element_type=jnp.float32
    )
    term_gain = jnp.sum(grad_normed * wide * inverse, axis=(0, 1))
    scaled = grad_normed * norm_gain
    grad_embedded = (
        inverse * scaled - wide * inverse**3 * jnp.sum(scaled * wide, axis=2, keepdims=True) / width
    )
    grad_embedded = grad_embedded + cotangent.astype(jnp.float32)
    term_embed = jnp.einsum("sct,std->cd", activated, grad_embedded, precision=HIGH)
    grad_mixed = jnp.einsum(
        "std,od->sot", grad_embedded, embed_weight, precision=HIGH
    ) * silu_slope(mixed)
    mixed_wide = extended(grad_mixed.astype(jnp.bfloat16), (("sites", 2),), 1).astype(
        grad_mixed.dtype
    )
    mix_terms = []
    grad_pooled = jnp.zeros(pooled.shape, jnp.float32)
    for shift_by in (-1, 0, 1):
        mix_terms.append(
            jnp.einsum(
                "sct,sot->co",
                pooled_wide[:, :, 1 + shift_by : 1 + shift_by + local],
                grad_mixed,
                precision=HIGH,
            )
        )
        grad_pooled = grad_pooled + jnp.einsum(
            "co,sot->sct",
            mix_weight[shift_by + 1],
            mixed_wide[:, :, 1 - shift_by : 1 - shift_by + local],
            precision=HIGH,
        )
    grad_pre = (grad_pooled / haps)[:, None] * silu_slope(pre)
    term_conv = jnp.einsum("shtk,shct->kc", patches, grad_pre, precision=HIGH)
    term_bias = jnp.sum(grad_pre, axis=(0, 1, 3))
    small = (term_conv, term_bias, jnp.stack(mix_terms), term_embed, term_gain)
    flat_small = lax.psum(jnp.concatenate([t.reshape(-1) for t in small]), ("sims", "sites"))
    pieces = []
    lower = 0
    for t in small:
        pieces.append(flat_small[lower : lower + t.size].reshape(t.shape))
        lower += t.size
    grad_conv, grad_bias, grad_mix, grad_embed, grad_gain = pieces
    return (grad_attention, grad_conv, grad_bias, grad_mix, grad_embed, grad_gain)


def solution(mesh):
    placed = (
        P("sims", None, "sites"),
        P("sims", "sites"),
        P("sims"),
        P("sims", "sites", None),
        P(),
        P(),
        P(),
        P(),
        P(),
        P(),
    )
    return jax.shard_map(
        per_device,
        mesh=mesh,
        in_specs=placed,
        out_specs=(P(("sims", "sites")), P(), P(), P(), P(), P()),
        check_vma=False,
    )
```

profile of v0, /device:TPU:8, one launch (start us, length us, event | category | flops | bytes accessed | tf_op | source)
XLA Modules:
  0.0 869.0 jit_solution(17943417780981665908)
XLA Ops:
  8.5 4.5 fusion.16
  13.1 13.1 %collective-permute-start.1 = (f32[1,64,1]{2,1,0:T(8,128)S(1)}, f32[1,64,1]{2,1,0:T(8,128)S(1)}, u32[]{:S(2)}, u32[]{:S(2)}) collective-permute-start(f32[1,64,1]{2,1,0:T(8,128)S(1)} %get-tuple-element.31), channel_id=1, source_target_pairs={{1,0},{2,1},{3,2},{4,3},{5,4},{6,5},{7,6},{8,7},{9,8},{10,9},{11,1... | collective-permute-start | bytes 776 | tf_op jit(solution)/shard_map/ppermute | solution.py:22
  30.2 6.0 collective-permute-done
  42.0 4.6 collective-permute-start.3
  48.6 7.8 collective-permute-start.5
  58.7 9.6 %collective-permute-done.2 = bf16[1,128,1025]{2,1,0:T(8,128)(2,1)} collective-permute-done((bf16[1,128,1025]{2,1,0:T(8,128)(2,1)}, bf16[1,128,1025]{2,1,0:T(8,128)(2,1)}, u32[]{:S(2)}, u32[]{:S(2)}) %collective-permute-start.2) | collective-permute-done | bytes 262432 | tf_op jit(solution)/shard_map/ppermute | solution.py:32
  71.9 2.8 collective-permute-start.8
  76.4 3.8 collective-permute-done.4
  80.3 15.8 %collective-permute-start.9 = (bf16[1,128,1025]{2,1,0:T(8,128)(2,1)}, bf16[1,128,1025]{2,1,0:T(8,128)(2,1)S(1)}, u32[]{:S(2)}, u32[]{:S(2)}) collective-permute-start(bf16[1,128,1025]{2,1,0:T(8,128)(2,1)} %get-tuple-element.28), channel_id=1, source_target_pairs={{0,4},{1,5},{2,6},{3,7},{4,8},{5,9},{6,10},{7,11},{8,12},{9,13},{1... | collective-permute-start | bytes 787208 | tf_op jit(solution)/shard_map/ppermute | solution.py:32
  103.6 2.8 fusion.114
  118.3 6.1 collective-permute-start.10
  124.4 4.0 collective-permute-start.11
  128.5 4.2 collective-permute-start.12
  132.7 7.7 collective-permute-start.13
  142.5 6.9 collective-permute-start.15
  151.7 4.8 collective-permute-start.17
  160.4 4.4 collective-permute-done.14
  166.6 3.1 copy.52
  174.2 9.6 %collective-permute-start.19 = (bf16[1,64,1]{2,1,0:T(8,128)(2,1)S(1)}, bf16[1,64,1]{2,1,0:T(8,128)(2,1)S(1)}, u32[]{:S(2)}, u32[]{:S(2)}) collective-permute-start(bf16[1,64,1]{2,1,0:T(8,128)(2,1)S(1)} %get-tuple-element.33), channel_id=1, source_target_pairs={{0,1},{1,2},{2,3},{3,4},{4,5},{5,6},{6,7},{7,8},{8,9},{9,10},{10,1... | collective-permute-start | bytes 392 | tf_op jit(solution)/shard_map/ppermute | solution.py:20
  186.1 4.4 collective-permute-done.18
  190.8 2.4 fusion.30
  197.0 225.5 %all-reduce.8.cloned.1.call-done = f32[1048576]{0:T(1024)} async-done(((f32[1048576]{0:T(1024)}), f32[1048576]{0:T(1024)}) %all-reduce.8.cloned.1.call-update) | async-done | bytes 4194320
  426.0 267.0 %all-reduce.6.cloned.1.call-done = f32[45888]{0:T(1024)} async-done(((f32[45888]{0:T(1024)}), f32[45888]{0:T(1024)}) %all-reduce.6.cloned.1.call-update) | async-done | bytes 183568 | tf_op jit(solution)/shard_map/psum | solution.py:229
  700.2 161.0 %all-reduce.10.cloned.1.call-done = f32[32768]{0:T(1024)} async-done(((f32[32768]{0:T(1024)}), f32[32768]{0:T(1024)}) %all-reduce.10.cloned.1.call-update) | async-done | bytes 131088
  (170 shorter events, 70.3 us)
Async XLA Ops:
  7.2 415.3 %all-reduce.8.cloned.1.call-start = ((), (), s32[]{:S(2)}) async-start(), calls=%async_computation.1 | async-start | bytes 8388608
  8.5 29.6 %copy-start.1 = (bf16[4,512,512]{2,1,0:T(8,128)(2,1)S(1)}, bf16[4,512,512]{2,1,0:T(8,128)(2,1)}, u32[]{:S(2)}) copy-start(bf16[4,512,512]{2,1,0:T(8,128)(2,1)} %param.19) | copy-start | bytes 6291460
  13.1 16.8 %collective-permute-start.1 = (f32[1,64,1]{2,1,0:T(8,128)S(1)}, f32[1,64,1]{2,1,0:T(8,128)S(1)}, u32[]{:S(2)}, u32[]{:S(2)}) collective-permute-start(f32[1,64,1]{2,1,0:T(8,128)S(1)} %get-tuple-element.31), channel_id=1, source_target_pairs={{1,0},{2,1},{3,2},{4,3},{5,4},{6,5},{7,6},{8,7},{9,8},{10,9},{11,1... | collective-permute-start | bytes 776 | tf_op jit(solution)/shard_map/ppermute | solution.py:22
  26.3 10.0 %collective-permute-start = (f32[1,64,1]{2,1,0:T(8,128)S(1)}, f32[1,64,1]{2,1,0:T(8,128)S(1)}, u32[]{:S(2)}, u32[]{:S(2)}) collective-permute-start(f32[1,64,1]{2,1,0:T(8,128)S(1)} %get-tuple-element.30), channel_id=1, source_target_pairs={{0,1},{1,2},{2,3},{3,4},{4,5},{5,6},{6,7},{7,8},{8,9},{9,10},{10,1... | collective-permute-start | bytes 776 | tf_op jit(solution)/shard_map/ppermute | solution.py:20
  39.5 28.8 %collective-permute-start.2 = (bf16[1,128,1025]{2,1,0:T(8,128)(2,1)}, bf16[1,128,1025]{2,1,0:T(8,128)(2,1)}, u32[]{:S(2)}, u32[]{:S(2)}) collective-permute-start(bf16[1,128,1025]{2,1,0:T(8,128)(2,1)} %get-tuple-element.28), channel_id=1, source_target_pairs={{0,15},{1,0},{2,1},{3,2},{4,3},{5,4},{6,5},{7,6},{8,7},{9,8},{10,9... | collective-permute-start | bytes 787208 | tf_op jit(solution)/shard_map/ppermute | solution.py:32
  42.0 29.9 %collective-permute-start.3 = (bf16[1,128,1025]{2,1,0:T(8,128)(2,1)}, bf16[1,128,1025]{2,1,0:T(8,128)(2,1)}, u32[]{:S(2)}, u32[]{:S(2)}) collective-permute-start(bf16[1,128,1025]{2,1,0:T(8,128)(2,1)} %get-tuple-element.28), channel_id=1, source_target_pairs={{0,1},{1,2},{2,3},{3,4},{4,5},{5,6},{6,7},{7,8},{8,9},{9,10},{10,1... | collective-permute-start | bytes 787208 | tf_op jit(solution)/shard_map/ppermute | solution.py:32
  46.7 33.6 %collective-permute-start.4 = (bf16[1,128,1025]{2,1,0:T(8,128)(2,1)}, bf16[1,128,1025]{2,1,0:T(8,128)(2,1)}, u32[]{:S(2)}, u32[]{:S(2)}) collective-permute-start(bf16[1,128,1025]{2,1,0:T(8,128)(2,1)} %get-tuple-element.28), channel_id=1, source_target_pairs={{0,14},{1,15},{2,0},{3,1},{4,2},{5,3},{6,4},{7,5},{8,6},{9,7},{10,... | collective-permute-start | bytes 787208 | tf_op jit(solution)/shard_map/ppermute | solution.py:32
  48.6 49.2 %collective-permute-start.5 = (bf16[1,128,1025]{2,1,0:T(8,128)(2,1)}, bf16[1,128,1025]{2,1,0:T(8,128)(2,1)}, u32[]{:S(2)}, u32[]{:S(2)}) collective-permute-start(bf16[1,128,1025]{2,1,0:T(8,128)(2,1)} %get-tuple-element.28), channel_id=1, source_target_pairs={{0,2},{1,3},{2,4},{3,5},{4,6},{5,7},{6,8},{7,9},{8,10},{9,11},{10,... | collective-permute-start | bytes 787208 | tf_op jit(solution)/shard_map/ppermute | solution.py:32
  56.4 43.0 %collective-permute-start.6 = (bf16[1,128,1025]{2,1,0:T(8,128)(2,1)}, bf16[1,128,1025]{2,1,0:T(8,128)(2,1)}, u32[]{:S(2)}, u32[]{:S(2)}) collective-permute-start(bf16[1,128,1025]{2,1,0:T(8,128)(2,1)} %get-tuple-element.28), channel_id=1, source_target_pairs={{0,13},{1,14},{2,15},{3,0},{4,1},{5,2},{6,3},{7,4},{8,5},{9,6},{10... | collective-permute-start | bytes 787208 | tf_op jit(solution)/shard_map/ppermute | solution.py:32
  68.3 32.9 %collective-permute-start.7 = (bf16[1,128,1025]{2,1,0:T(8,128)(2,1)}, bf16[1,128,1025]{2,1,0:T(8,128)(2,1)S(1)}, u32[]{:S(2)}, u32[]{:S(2)}) collective-permute-start(bf16[1,128,1025]{2,1,0:T(8,128)(2,1)} %get-tuple-element.28), channel_id=1, source_target_pairs={{0,3},{1,4},{2,5},{3,6},{4,7},{5,8},{6,9},{7,10},{8,11},{9,12},{10... | collective-permute-start | bytes 787208 | tf_op jit(solution)/shard_map/ppermute | solution.py:32
  71.9 30.0 %collective-permute-start.8 = (bf16[1,128,1025]{2,1,0:T(8,128)(2,1)}, bf16[1,128,1025]{2,1,0:T(8,128)(2,1)S(1)}, u32[]{:S(2)}, u32[]{:S(2)}) collective-permute-start(bf16[1,128,1025]{2,1,0:T(8,128)(2,1)} %get-tuple-element.28), channel_id=1, source_target_pairs={{0,12},{1,13},{2,14},{3,15},{4,0},{5,1},{6,2},{7,3},{8,4},{9,5},{1... | collective-permute-start | bytes 787208 | tf_op jit(solution)/shard_map/ppermute | solution.py:32
  80.3 22.6 %collective-permute-start.9 = (bf16[1,128,1025]{2,1,0:T(8,128)(2,1)}, bf16[1,128,1025]{2,1,0:T(8,128)(2,1)S(1)}, u32[]{:S(2)}, u32[]{:S(2)}) collective-permute-start(bf16[1,128,1025]{2,1,0:T(8,128)(2,1)} %get-tuple-element.28), channel_id=1, source_target_pairs={{0,4},{1,5},{2,6},{3,7},{4,8},{5,9},{6,10},{7,11},{8,12},{9,13},{1... | collective-permute-start | bytes 787208 | tf_op jit(solution)/shard_map/ppermute | solution.py:32
  118.3 24.1 %collective-permute-start.10 = (bf16[1,128,16,64]{1,3,2,0:T(8,128)(2,1)S(1)}, bf16[1,128,16,64]{1,3,2,0:T(8,128)(2,1)S(1)}, u32[]{:S(2)}, u32[]{:S(2)}) collective-permute-start(bf16[1,128,16,64]{1,3,2,0:T(8,128)(2,1)S(1)} %pad_maximum_fusion.2), channel_id=1, source_target_pairs={{0,1},{1,2},{2,3},{3,4},{4,5},{5,6},{6,7},{7,8},{8,9},{9,10},{10,1... | collective-permute-start | bytes 786440 | tf_op jit(solution)/shard_map/ppermute | solution.py:32
  124.4 25.0 %collective-permute-start.11 = (bf16[1,128,16,64]{1,3,2,0:T(8,128)(2,1)S(1)}, bf16[1,128,16,64]{1,3,2,0:T(8,128)(2,1)S(1)}, u32[]{:S(2)}, u32[]{:S(2)}) collective-permute-start(bf16[1,128,16,64]{1,3,2,0:T(8,128)(2,1)S(1)} %pad_maximum_fusion.3), channel_id=1, source_target_pairs={{0,15},{1,0},{2,1},{3,2},{4,3},{5,4},{6,5},{7,6},{8,7},{9,8},{10,9... | collective-permute-start | bytes 786440 | tf_op jit(solution)/shard_map/ppermute | solution.py:32
  128.5 23.2 %collective-permute-start.12 = (bf16[1,128,16,64]{1,3,2,0:T(8,128)(2,1)S(1)}, bf16[1,128,16,64]{1,3,2,0:T(8,128)(2,1)S(1)}, u32[]{:S(2)}, u32[]{:S(2)}) collective-permute-start(bf16[1,128,16,64]{1,3,2,0:T(8,128)(2,1)S(1)} %pad_maximum_fusion.4), channel_id=1, source_target_pairs={{0,2},{1,3},{2,4},{3,5},{4,6},{5,7},{6,8},{7,9},{8,10},{9,11},{10,... | collective-permute-start | bytes 786440 | tf_op jit(solution)/shard_map/ppermute | solution.py:32
  132.7 27.7 %collective-permute-start.13 = (bf16[1,128,16,64]{1,3,2,0:T(8,128)(2,1)S(1)}, bf16[1,128,16,64]{1,3,2,0:T(8,128)(2,1)S(1)}, u32[]{:S(2)}, u32[]{:S(2)}) collective-permute-start(bf16[1,128,16,64]{1,3,2,0:T(8,128)(2,1)S(1)} %pad_maximum_fusion.5), channel_id=1, source_target_pairs={{0,14},{1,15},{2,0},{3,1},{4,2},{5,3},{6,4},{7,5},{8,6},{9,7},{10,... | collective-permute-start | bytes 786440 | tf_op jit(solution)/shard_map/ppermute | solution.py:32
  140.4 24.4 %collective-permute-start.14 = (bf16[1,128,16,64]{1,3,2,0:T(8,128)(2,1)S(1)}, bf16[1,128,16,64]{1,3,2,0:T(8,128)(2,1)S(1)}, u32[]{:S(2)}, u32[]{:S(2)}) collective-permute-start(bf16[1,128,16,64]{1,3,2,0:T(8,128)(2,1)S(1)} %pad_maximum_fusion.6), channel_id=1, source_target_pairs={{0,3},{1,4},{2,5},{3,6},{4,7},{5,8},{6,9},{7,10},{8,11},{9,12},{10... | collective-permute-start | bytes 786440 | tf_op jit(solution)/shard_map/ppermute | solution.py:32
  142.5 22.4 %collective-permute-start.15 = (bf16[1,128,16,64]{1,3,2,0:T(8,128)(2,1)S(1)}, bf16[1,128,16,64]{1,3,2,0:T(8,128)(2,1)S(1)}, u32[]{:S(2)}, u32[]{:S(2)}) collective-permute-start(bf16[1,128,16,64]{1,3,2,0:T(8,128)(2,1)S(1)} %pad_maximum_fusion.7), channel_id=1, source_target_pairs={{0,13},{1,14},{2,15},{3,0},{4,1},{5,2},{6,3},{7,4},{8,5},{9,6},{10... | collective-permute-start | bytes 786440 | tf_op jit(solution)/shard_map/ppermute | solution.py:32
  149.4 15.5 %collective-permute-start.16 = (bf16[1,128,16,64]{1,3,2,0:T(8,128)(2,1)S(1)}, bf16[1,128,16,64]{1,3,2,0:T(8,128)(2,1)S(1)}, u32[]{:S(2)}, u32[]{:S(2)}) collective-permute-start(bf16[1,128,16,64]{1,3,2,0:T(8,128)(2,1)S(1)} %pad_maximum_fusion.8), channel_id=1, source_target_pairs={{0,4},{1,5},{2,6},{3,7},{4,8},{5,9},{6,10},{7,11},{8,12},{9,13},{1... | collective-permute-start | bytes 786440 | tf_op jit(solution)/shard_map/ppermute | solution.py:32
  151.7 13.2 %collective-permute-start.17 = (bf16[1,128,16,64]{1,3,2,0:T(8,128)(2,1)S(1)}, bf16[1,128,16,64]{1,3,2,0:T(8,128)(2,1)S(1)}, u32[]{:S(2)}, u32[]{:S(2)}) collective-permute-start(bf16[1,128,16,64]{1,3,2,0:T(8,128)(2,1)S(1)} %pad_maximum_fusion.9), channel_id=1, source_target_pairs={{0,12},{1,13},{2,14},{3,15},{4,0},{5,1},{6,2},{7,3},{8,4},{9,5},{1... | collective-permute-start | bytes 786440 | tf_op jit(solution)/shard_map/ppermute | solution.py:32
  169.8 523.3 %all-reduce.6.cloned.1.call-start = ((), (), s32[]{:S(2)}) async-start(), calls=%async_computation | async-start | bytes 368640 | tf_op jit(solution)/shard_map/psum | solution.py:229
  174.2 11.7 %collective-permute-start.19 = (bf16[1,64,1]{2,1,0:T(8,128)(2,1)S(1)}, bf16[1,64,1]{2,1,0:T(8,128)(2,1)S(1)}, u32[]{:S(2)}, u32[]{:S(2)}) collective-permute-start(bf16[1,64,1]{2,1,0:T(8,128)(2,1)S(1)} %get-tuple-element.33), channel_id=1, source_target_pairs={{0,1},{1,2},{2,3},{3,4},{4,5},{5,6},{6,7},{7,8},{8,9},{9,10},{10,1... | collective-permute-start | bytes 392 | tf_op jit(solution)/shard_map/ppermute | solution.py:20
  184.0 6.5 collective-permute-start.18
  195.1 666.1 %all-reduce.10.cloned.1.call-start = ((), (), s32[]{:S(2)}) async-start(), calls=%async_computation.2 | async-start | bytes 262144
  (17 other events, 214.3 us)
Sparse Core Ops, SparseCore 0:
  169.9 252.5 all-reduce.7
  427.5 265.5 all-reduce.5
  696.2 164.9 all-reduce.9
where the time goes:
time: 870 us; the launch traced here: 869 us
  waiting for transfers between devices  684 us (79%)
  starting transfers between devices  104 us (12%)
  local copies, waits for them, and re-layouts  35.6 us (4%)
  matrix products  19.2 us (2%)
  between operations  16.8 us (2%)
  other arithmetic  9.7 us (1%)
    unnamed x5, waiting for transfers between devices  386 us
    psum x1, waiting for transfers between devices, per_device(): lax.psum(jnp.concatenate([t.reshape(-1) for t in small]), ('sims', 'sites'))  267 us
    ppermute x16, starting transfers between devices, from_behind(): return lax.ppermute(value, axis, pairs)  76.7 us
    unnamed x49, local copies, waits for them, and re-layouts  20.3 us
    ppermute x16, waiting for transfers between devices, from_behind(): return lax.ppermute(value, axis, pairs)  20.2 us
  transfers between devices with their start and end apart: 23, of which 10 were waited for; matrix products, arithmetic and copies ran while one was open for 4% of the time, Pallas kernels for 0%

commit v1 on v0

--- a/solution.py
+++ b/solution.py
@@ -226,7 +226,9 @@
     term_conv = jnp.einsum("shtk,shct->kc", patches, grad_pre, precision=HIGH)
     term_bias = jnp.sum(grad_pre, axis=(0, 1, 3))
     small = (term_conv, term_bias, jnp.stack(mix_terms), term_embed, term_gain)
-    flat_small = lax.psum(jnp.concatenate([t.reshape(-1) for t in small]), ("sims", "sites"))
+    flat_small = lax.psum(
+        lax.psum(jnp.concatenate([t.reshape(-1) for t in small]), "sites"), "sims"
+    )
     pieces = []
     lower = 0
     for t in small:

time: 870 us -> 796 us (0.915)
  waiting for transfers between devices: 684 us -> 598 us
    psum x1, waiting for transfers between devices: 267 us -> 171 us  [per_device(): lax.psum(jnp.concatenate([t.reshape(-1) for t in small]), 'sites')]
    unnamed x5, waiting for transfers between devices: 386 us -> 401 us
    unnamed x49 -> x45, local copies, waits for them, and re-layouts: 20.3 us -> 19.3 us
where the time goes in v1:
time: 796 us; the launch traced here: 794 us
  waiting for transfers between devices  598 us (75%)
  starting transfers between devices  108 us (14%)
  local copies, waits for them, and re-layouts  35.8 us (4%)
  matrix products  23.6 us (3%)
  between operations  16.7 us (2%)
  other arithmetic  11.4 us (1%)
    unnamed x5, waiting for transfers between devices  401 us
    psum x1, waiting for transfers between devices, per_device(): lax.psum(jnp.concatenate([t.reshape(-1) for t in small]), 'sites')  171 us
    ppermute x16, starting transfers between devices, from_behind(): return lax.ppermute(value, axis, pairs)  82.9 us
    unnamed x45, local copies, waits for them, and re-layouts  19.3 us
    ppermute x16, waiting for transfers between devices, from_behind(): return lax.ppermute(value, axis, pairs)  18.7 us
    ppermute x2, starting transfers between devices, extended(): lax.ppermute(head, axis, [((i + 1) % count, i) for i in range(count)])  17.8 us
  transfers between devices with their start and end apart: 23, of which 10 were waited for; matrix products, arithmetic and copies ran while one was open for 4% of the time, Pallas kernels for 0%

profile of v1, /device:TPU:8, one launch (start us, length us, event | category | flops | bytes accessed | tf_op | source)
XLA Modules:
  0.0 794.0 jit_solution(5818837977827067071)
XLA Ops:
  9.1 4.5 fusion.16
  13.7 13.1 %collective-permute-start.1 = (f32[1,64,1]{2,1,0:T(8,128)S(1)}, f32[1,64,1]{2,1,0:T(8,128)S(1)}, u32[]{:S(2)}, u32[]{:S(2)}) collective-permute-start(f32[1,64,1]{2,1,0:T(8,128)S(1)} %get-tuple-element.33), channel_id=1, source_target_pairs={{1,0},{2,1},{3,2},{4,3},{5,4},{6,5},{7,6},{8,7},{9,8},{10,9},{11,1... | collective-permute-start | bytes 776 | tf_op jit(solution)/shard_map/ppermute | solution.py:22
  30.8 6.0 collective-permute-done
  41.7 4.6 collective-permute-start.3
  48.3 7.8 collective-permute-start.5
  58.4 6.0 collective-permute-start.7
  66.2 3.6 collective-permute-done.3
  69.7 4.6 collective-permute-start.8
  76.0 3.9 collective-permute-done.4
  79.9 15.8 %collective-permute-start.9 = (bf16[1,128,1025]{2,1,0:T(8,128)(2,1)}, bf16[1,128,1025]{2,1,0:T(8,128)(2,1)S(1)}, u32[]{:S(2)}, u32[]{:S(2)}) collective-permute-start(bf16[1,128,1025]{2,1,0:T(8,128)(2,1)} %get-tuple-element.30), channel_id=1, source_target_pairs={{0,4},{1,5},{2,6},{3,7},{4,8},{5,9},{6,10},{7,11},{8,12},{9,13},{1... | collective-permute-start | bytes 787208 | tf_op jit(solution)/shard_map/ppermute | solution.py:32
  117.7 6.1 collective-permute-start.10
  123.8 4.1 collective-permute-start.11
  128.0 4.2 collective-permute-start.12
  132.2 7.7 collective-permute-start.13
  142.4 6.9 collective-permute-start.15
  151.3 5.1 collective-permute-start.17
  159.9 8.3 %collective-permute-done.14 = bf16[1,128,16,64]{1,3,2,0:T(8,128)(2,1)S(1)} collective-permute-done((bf16[1,128,16,64]{1,3,2,0:T(8,128)(2,1)S(1)}, bf16[1,128,16,64]{1,3,2,0:T(8,128)(2,1)S(1)}, u32[]{:S(2)}, u32[]{:S(2)}) %collective-permute-start.14) | collective-permute-done | bytes 262176 | tf_op jit(solution)/shard_map/ppermute | solution.py:32
  176.4 5.7 collective-permute-start.19
  182.1 4.7 collective-permute-start.18
  192.5 3.1 fusion.30
  198.2 3.1 copy.52
  201.3 171.2 %all-reduce.7.cloned.1.call-done = f32[45888]{0:T(1024)} async-done(((f32[45888]{0:T(1024)}), f32[45888]{0:T(1024)}) %all-reduce.7.cloned.1.call-update) | async-done | bytes 183568 | tf_op jit(solution)/shard_map/psum | solution.py:230
  374.4 236.3 %all-reduce.11.cloned.1.call-done = (f32[1048576]{0:T(1024)}, f32[45888]{0:T(1024)}) async-done(((f32[1048576]{0:T(1024)}, f32[45888]{0:T(1024)}), (f32[1048576]{0:T(1024)}, f32[45888]{0:T(1024)})) %all-reduce.11.cloned.1.call-update) | async-done | bytes 4377872
  621.5 164.7 %all-reduce.9.cloned.1.call-done = f32[32768]{0:T(1024)} async-done(((f32[32768]{0:T(1024)}), f32[32768]{0:T(1024)}) %all-reduce.9.cloned.1.call-update) | async-done | bytes 131088
  (166 shorter events, 76.0 us)
Async XLA Ops:
  7.2 365.3 %all-reduce.7.cloned.1.call-start = ((), (), s32[]{:S(2)}) async-start(), calls=%async_computation | async-start | bytes 368640 | tf_op jit(solution)/shard_map/psum | solution.py:230
  13.7 16.8 %collective-permute-start.1 = (f32[1,64,1]{2,1,0:T(8,128)S(1)}, f32[1,64,1]{2,1,0:T(8,128)S(1)}, u32[]{:S(2)}, u32[]{:S(2)}) collective-permute-start(f32[1,64,1]{2,1,0:T(8,128)S(1)} %get-tuple-element.33), channel_id=1, source_target_pairs={{1,0},{2,1},{3,2},{4,3},{5,4},{6,5},{7,6},{8,7},{9,8},{10,9},{11,1... | collective-permute-start | bytes 776 | tf_op jit(solution)/shard_map/ppermute | solution.py:22
  26.9 10.0 %collective-permute-start = (f32[1,64,1]{2,1,0:T(8,128)S(1)}, f32[1,64,1]{2,1,0:T(8,128)S(1)}, u32[]{:S(2)}, u32[]{:S(2)}) collective-permute-start(f32[1,64,1]{2,1,0:T(8,128)S(1)} %get-tuple-element.32), channel_id=1, source_target_pairs={{0,1},{1,2},{2,3},{3,4},{4,5},{5,6},{6,7},{7,8},{8,9},{9,10},{10,1... | collective-permute-start | bytes 776 | tf_op jit(solution)/shard_map/ppermute | solution.py:20
  39.1 19.3 %collective-permute-start.2 = (bf16[1,128,1025]{2,1,0:T(8,128)(2,1)}, bf16[1,128,1025]{2,1,0:T(8,128)(2,1)}, u32[]{:S(2)}, u32[]{:S(2)}) collective-permute-start(bf16[1,128,1025]{2,1,0:T(8,128)(2,1)} %get-tuple-element.30), channel_id=1, source_target_pairs={{0,15},{1,0},{2,1},{3,2},{4,3},{5,4},{6,5},{7,6},{8,7},{9,8},{10,9... | collective-permute-start | bytes 787208 | tf_op jit(solution)/shard_map/ppermute | solution.py:32
  41.7 28.0 %collective-permute-start.3 = (bf16[1,128,1025]{2,1,0:T(8,128)(2,1)}, bf16[1,128,1025]{2,1,0:T(8,128)(2,1)}, u32[]{:S(2)}, u32[]{:S(2)}) collective-permute-start(bf16[1,128,1025]{2,1,0:T(8,128)(2,1)} %get-tuple-element.30), channel_id=1, source_target_pairs={{0,1},{1,2},{2,3},{3,4},{4,5},{5,6},{6,7},{7,8},{8,9},{9,10},{10,1... | collective-permute-start | bytes 787208 | tf_op jit(solution)/shard_map/ppermute | solution.py:32
  46.3 33.6 %collective-permute-start.4 = (bf16[1,128,1025]{2,1,0:T(8,128)(2,1)}, bf16[1,128,1025]{2,1,0:T(8,128)(2,1)}, u32[]{:S(2)}, u32[]{:S(2)}) collective-permute-start(bf16[1,128,1025]{2,1,0:T(8,128)(2,1)} %get-tuple-element.30), channel_id=1, source_target_pairs={{0,14},{1,15},{2,0},{3,1},{4,2},{5,3},{6,4},{7,5},{8,6},{9,7},{10,... | collective-permute-start | bytes 787208 | tf_op jit(solution)/shard_map/ppermute | solution.py:32
  48.3 49.2 %collective-permute-start.5 = (bf16[1,128,1025]{2,1,0:T(8,128)(2,1)}, bf16[1,128,1025]{2,1,0:T(8,128)(2,1)}, u32[]{:S(2)}, u32[]{:S(2)}) collective-permute-start(bf16[1,128,1025]{2,1,0:T(8,128)(2,1)} %get-tuple-element.30), channel_id=1, source_target_pairs={{0,2},{1,3},{2,4},{3,5},{4,6},{5,7},{6,8},{7,9},{8,10},{9,11},{10,... | collective-permute-start | bytes 787208 | tf_op jit(solution)/shard_map/ppermute | solution.py:32
  56.1 43.0 %collective-permute-start.6 = (bf16[1,128,1025]{2,1,0:T(8,128)(2,1)}, bf16[1,128,1025]{2,1,0:T(8,128)(2,1)}, u32[]{:S(2)}, u32[]{:S(2)}) collective-permute-start(bf16[1,128,1025]{2,1,0:T(8,128)(2,1)} %get-tuple-element.30), channel_id=1, source_target_pairs={{0,13},{1,14},{2,15},{3,0},{4,1},{5,2},{6,3},{7,4},{8,5},{9,6},{10... | collective-permute-start | bytes 787208 | tf_op jit(solution)/shard_map/ppermute | solution.py:32
  58.4 42.4 %collective-permute-start.7 = (bf16[1,128,1025]{2,1,0:T(8,128)(2,1)}, bf16[1,128,1025]{2,1,0:T(8,128)(2,1)S(1)}, u32[]{:S(2)}, u32[]{:S(2)}) collective-permute-start(bf16[1,128,1025]{2,1,0:T(8,128)(2,1)} %get-tuple-element.30), channel_id=1, source_target_pairs={{0,3},{1,4},{2,5},{3,6},{4,7},{5,8},{6,9},{7,10},{8,11},{9,12},{10... | collective-permute-start | bytes 787208 | tf_op jit(solution)/shard_map/ppermute | solution.py:32
  69.7 31.9 %collective-permute-start.8 = (bf16[1,128,1025]{2,1,0:T(8,128)(2,1)}, bf16[1,128,1025]{2,1,0:T(8,128)(2,1)S(1)}, u32[]{:S(2)}, u32[]{:S(2)}) collective-permute-start(bf16[1,128,1025]{2,1,0:T(8,128)(2,1)} %get-tuple-element.30), channel_id=1, source_target_pairs={{0,12},{1,13},{2,14},{3,15},{4,0},{5,1},{6,2},{7,3},{8,4},{9,5},{1... | collective-permute-start | bytes 787208 | tf_op jit(solution)/shard_map/ppermute | solution.py:32
  79.9 22.6 %collective-permute-start.9 = (bf16[1,128,1025]{2,1,0:T(8,128)(2,1)}, bf16[1,128,1025]{2,1,0:T(8,128)(2,1)S(1)}, u32[]{:S(2)}, u32[]{:S(2)}) collective-permute-start(bf16[1,128,1025]{2,1,0:T(8,128)(2,1)} %get-tuple-element.30), channel_id=1, source_target_pairs={{0,4},{1,5},{2,6},{3,7},{4,8},{5,9},{6,10},{7,11},{8,12},{9,13},{1... | collective-permute-start | bytes 787208 | tf_op jit(solution)/shard_map/ppermute | solution.py:32
  117.7 24.7 %collective-permute-start.10 = (bf16[1,128,16,64]{1,3,2,0:T(8,128)(2,1)S(1)}, bf16[1,128,16,64]{1,3,2,0:T(8,128)(2,1)S(1)}, u32[]{:S(2)}, u32[]{:S(2)}) collective-permute-start(bf16[1,128,16,64]{1,3,2,0:T(8,128)(2,1)S(1)} %pad_maximum_fusion.2), channel_id=1, source_target_pairs={{0,1},{1,2},{2,3},{3,4},{4,5},{5,6},{6,7},{7,8},{8,9},{9,10},{10,1... | collective-permute-start | bytes 786440 | tf_op jit(solution)/shard_map/ppermute | solution.py:32
  123.8 32.6 %copy-start.5 = (bf16[1,128,512]{2,1,0:T(8,128)(2,1)S(1)}, bf16[1,128,512]{2,1,0:T(8,128)(2,1)}, u32[]{:S(2)}) copy-start(bf16[1,128,512]{2,1,0:T(8,128)(2,1)} %param.13) | copy-start | bytes 393220
  123.8 25.5 %collective-permute-start.11 = (bf16[1,128,16,64]{1,3,2,0:T(8,128)(2,1)S(1)}, bf16[1,128,16,64]{1,3,2,0:T(8,128)(2,1)S(1)}, u32[]{:S(2)}, u32[]{:S(2)}) collective-permute-start(bf16[1,128,16,64]{1,3,2,0:T(8,128)(2,1)S(1)} %pad_maximum_fusion.3), channel_id=1, source_target_pairs={{0,15},{1,0},{2,1},{3,2},{4,3},{5,4},{6,5},{7,6},{8,7},{9,8},{10,9... | collective-permute-start | bytes 786440 | tf_op jit(solution)/shard_map/ppermute | solution.py:32
  128.0 23.3 %collective-permute-start.12 = (bf16[1,128,16,64]{1,3,2,0:T(8,128)(2,1)S(1)}, bf16[1,128,16,64]{1,3,2,0:T(8,128)(2,1)S(1)}, u32[]{:S(2)}, u32[]{:S(2)}) collective-permute-start(bf16[1,128,16,64]{1,3,2,0:T(8,128)(2,1)S(1)} %pad_maximum_fusion.4), channel_id=1, source_target_pairs={{0,2},{1,3},{2,4},{3,5},{4,6},{5,7},{6,8},{7,9},{8,10},{9,11},{10,... | collective-permute-start | bytes 786440 | tf_op jit(solution)/shard_map/ppermute | solution.py:32
  132.2 27.7 %collective-permute-start.13 = (bf16[1,128,16,64]{1,3,2,0:T(8,128)(2,1)S(1)}, bf16[1,128,16,64]{1,3,2,0:T(8,128)(2,1)S(1)}, u32[]{:S(2)}, u32[]{:S(2)}) collective-permute-start(bf16[1,128,16,64]{1,3,2,0:T(8,128)(2,1)S(1)} %pad_maximum_fusion.5), channel_id=1, source_target_pairs={{0,14},{1,15},{2,0},{3,1},{4,2},{5,3},{6,4},{7,5},{8,6},{9,7},{10,... | collective-permute-start | bytes 786440 | tf_op jit(solution)/shard_map/ppermute | solution.py:32
  139.9 28.3 %collective-permute-start.14 = (bf16[1,128,16,64]{1,3,2,0:T(8,128)(2,1)S(1)}, bf16[1,128,16,64]{1,3,2,0:T(8,128)(2,1)S(1)}, u32[]{:S(2)}, u32[]{:S(2)}) collective-permute-start(bf16[1,128,16,64]{1,3,2,0:T(8,128)(2,1)S(1)} %pad_maximum_fusion.6), channel_id=1, source_target_pairs={{0,3},{1,4},{2,5},{3,6},{4,7},{5,8},{6,9},{7,10},{8,11},{9,12},{10... | collective-permute-start | bytes 786440 | tf_op jit(solution)/shard_map/ppermute | solution.py:32
  142.4 25.9 %collective-permute-start.15 = (bf16[1,128,16,64]{1,3,2,0:T(8,128)(2,1)S(1)}, bf16[1,128,16,64]{1,3,2,0:T(8,128)(2,1)S(1)}, u32[]{:S(2)}, u32[]{:S(2)}) collective-permute-start(bf16[1,128,16,64]{1,3,2,0:T(8,128)(2,1)S(1)} %pad_maximum_fusion.7), channel_id=1, source_target_pairs={{0,13},{1,14},{2,15},{3,0},{4,1},{5,2},{6,3},{7,4},{8,5},{9,6},{10... | collective-permute-start | bytes 786440 | tf_op jit(solution)/shard_map/ppermute | solution.py:32
  149.4 19.0 %collective-permute-start.16 = (bf16[1,128,16,64]{1,3,2,0:T(8,128)(2,1)S(1)}, bf16[1,128,16,64]{1,3,2,0:T(8,128)(2,1)S(1)}, u32[]{:S(2)}, u32[]{:S(2)}) collective-permute-start(bf16[1,128,16,64]{1,3,2,0:T(8,128)(2,1)S(1)} %pad_maximum_fusion.8), channel_id=1, source_target_pairs={{0,4},{1,5},{2,6},{3,7},{4,8},{5,9},{6,10},{7,11},{8,12},{9,13},{1... | collective-permute-start | bytes 786440 | tf_op jit(solution)/shard_map/ppermute | solution.py:32
  151.3 17.1 %collective-permute-start.17 = (bf16[1,128,16,64]{1,3,2,0:T(8,128)(2,1)S(1)}, bf16[1,128,16,64]{1,3,2,0:T(8,128)(2,1)S(1)}, u32[]{:S(2)}, u32[]{:S(2)}) collective-permute-start(bf16[1,128,16,64]{1,3,2,0:T(8,128)(2,1)S(1)} %pad_maximum_fusion.9), channel_id=1, source_target_pairs={{0,12},{1,13},{2,14},{3,15},{4,0},{5,1},{6,2},{7,3},{8,4},{9,5},{1... | collective-permute-start | bytes 786440 | tf_op jit(solution)/shard_map/ppermute | solution.py:32
  176.4 10.4 %collective-permute-start.19 = (bf16[1,64,1]{2,1,0:T(8,128)(2,1)}, bf16[1,64,1]{2,1,0:T(8,128)(2,1)S(1)}, u32[]{:S(2)}, u32[]{:S(2)}) collective-permute-start(bf16[1,64,1]{2,1,0:T(8,128)(2,1)} %get-tuple-element.35), channel_id=1, source_target_pairs={{0,1},{1,2},{2,3},{3,4},{4,5},{5,6},{6,7},{7,8},{8,9},{9,10},{10,1... | collective-permute-start | bytes 392 | tf_op jit(solution)/shard_map/ppermute | solution.py:20
  182.1 6.7 collective-permute-start.18
  196.5 414.3 %all-reduce.11.cloned.1.call-start = ((), (), s32[]{:S(2)}) async-start(), calls=%async_computation.2 | async-start | bytes 8757248
  372.5 413.7 %all-reduce.9.cloned.1.call-start = ((), (), s32[]{:S(2)}) async-start(), calls=%async_computation.1 | async-start | bytes 262144
  (15 other events, 240.1 us)
Sparse Core Ops, SparseCore 0:
  196.6 175.8 all-reduce.6
  375.8 234.9 all-reduce.10
  613.7 172.4 all-reduce.8
